TPU v7x, 32 devices: a whole 2x2x4 slice. The times are simulated.
32 devices in a mesh: chan: 8 (over z, y), win: 4 (over x, core).
Axes of the slice: x: 2, y: 2, z: 4, core: 2. Of those that a mesh axis runs over, the one named last changes fastest.
Arguments:
- samples: bfloat16 [8, 256, 6144], P('win', 'chan'), may hold values from -6 to 6
- pair_offsets: int32 [8, 3], P('chan'), may hold values from 0 to 2, each once within a row
- spectral_slot_position: int32 [1024], replicated, may hold values from 1 to 3071, as said below
Outputs:
- correlations: float32 [256, 3, 2, 32, 1024], P('chan', None, None, None, 'win')
Inputs may be any that keep to these rules, and one draw needn't show every extreme that they name: `pair_offsets`: each row holds every offset of 0 to 2 once. `spectral_slot_position`: distinct and rising; the first is 1 and the last is 3071.
All inputs are finite; a program needn't handle non-finite values.
Results may differ from a plain program's by a relative error of at most 0.0036.
Values sent between devices are 32-bit elements; how exact they have to be, the bound alone decides.
No kernel may reach another device: no remote copies, remote signals or barrier semaphores. Data moves between devices by JAX's collectives and lax.ppermute only.
A program may use at most 64 MiB of HBM per device.

v0:
```python
import math
import jax
import jax.numpy as jnp
from jax import lax
from jax.sharding import PartitionSpec as P

S = 6144
HALF = 64
TB = 1024
EPSILON = 1e-06


def passed_along(value, axis, steps):
    count = lax.axis_size(axis)
    leading, last = (max(0, -steps), min(count, count - steps))
    return lax.ppermute(value, axis, [(source, source + steps) for source in range(leading, last)])


def angle_parts(spectral_slot_position):
    factor = 2.0 * math.pi / S
    moments = jnp.arange(TB, dtype=jnp.int32)
    base = (moments[:, None] * spectral_slot_position[None, :] % S).astype(jnp.float32) * factor
    starts = jnp.arange(S // TB, dtype=jnp.int32) * TB
    turns = (starts[:, None] * spectral_slot_position[None, :] % S).astype(jnp.float32) * factor
    return (jnp.cos(base), jnp.sin(base), jnp.cos(turns), jnp.sin(turns))


def block_table(base_cos, base_sin, turn_cos, turn_sin):
    scale = 1.0 / math.sqrt(S)
    cos_part = (base_cos * turn_cos - base_sin * turn_sin) * scale
    sin_part = (base_sin * turn_cos + base_cos * turn_sin) * scale
    return jnp.concatenate([cos_part, sin_part], axis=-1).astype(jnp.bfloat16)


def whiten(spectra, half_width):
    freq_count = spectra.shape[-1]
    powers = spectra[..., 0, :] * spectra[..., 0, :] + spectra[..., 1, :] * spectra[..., 1, :]
    places = jnp.arange(freq_count, dtype=jnp.int32)
    banded = (jnp.abs(places[:, None] - places[None, :]) <= half_width).astype(jnp.float32)
    tallies = jnp.sum(banded, axis=0)
    flattened = powers.reshape(-1, freq_count)
    smoothed_amplitude = (
        jnp.dot(flattened, banded, precision=lax.Precision.HIGHEST).reshape(powers.shape) / tallies
    )
    amplitude = jnp.sqrt(smoothed_amplitude + EPSILON)
    return spectra / amplitude[..., None, :]


def arrange(field):
    win_count, chan_count, _, freq_count = field.shape
    return field.transpose(3, 1, 0, 2).reshape(freq_count, chan_count, win_count * 2)


def pair_blocks(spectra, offsets, windows):
    nearer = passed_along(spectra, "chan", 1)
    farther = passed_along(spectra, "chan", 2)
    win_count, chan_count, _, freq_count = spectra.shape
    flipped = jnp.stack([spectra[:, :, 1], -spectra[:, :, 0]], axis=2)
    left = jnp.concatenate([arrange(spectra), arrange(flipped)], axis=1)
    right = jnp.concatenate([arrange(spectra), arrange(nearer), arrange(farther)], axis=1)
    joined = jnp.einsum("fik,fjk->fij", left, right, precision=lax.Precision.HIGHEST) / windows
    joined = joined.reshape(freq_count, 2, chan_count, 3, chan_count)
    slots = []
    for position in range(offsets.shape[0]):
        chosen = offsets[position]
        slots.append(
            jnp.where(
                chosen == 0,
                joined[:, :, :, 0],
                jnp.where(chosen == 1, joined[:, :, :, 1], joined[:, :, :, 2]),
            )
        )
    stacked = jnp.stack(slots, axis=0)
    return stacked.transpose(3, 0, 2, 4, 1)


def shards(samples, pair_offsets, spectral_slot_position):
    win_count, sensor_total, segment_span = samples.shape
    freq_count = spectral_slot_position.shape[0]
    time_series = samples.reshape(win_count * sensor_total, segment_span)
    base_cos, base_sin, turn_cos, turn_sin = angle_parts(spectral_slot_position)

    def add_block(step, total):
        piece = lax.dynamic_slice_in_dim(time_series, step * TB, TB, 1)
        row_cos = lax.dynamic_slice_in_dim(turn_cos, step, 1, 0)
        row_sin = lax.dynamic_slice_in_dim(turn_sin, step, 1, 0)
        table = block_table(base_cos, base_sin, row_cos, row_sin)
        return total + jnp.dot(piece, table, preferred_element_type=jnp.float32)

    initial = jnp.zeros((win_count * sensor_total, 2 * freq_count), jnp.float32)
    raw_parts = lax.fori_loop(0, segment_span // TB, add_block, initial)
    spectra = jnp.stack([raw_parts[:, :freq_count], -raw_parts[:, freq_count:]], axis=1)
    spectra = spectra.reshape(win_count, sensor_total, 2, freq_count)
    whitened = whiten(spectra, HALF)
    offsets = pair_offsets[0]
    slabs = lax.all_to_all(whitened, "win", split_axis=3, concat_axis=0, tiled=True)
    return pair_blocks(slabs, offsets, slabs.shape[0])


def solution(mesh):
    in_specs = (P("win", "chan", None), P("chan", None), P())
    out_specs = P("chan", None, None, None, "win")
    return jax.shard_map(shards, mesh=mesh, in_specs=in_specs, out_specs=out_specs, check_vma=False)
```

profile of v0, /device:TPU:28, one launch (start us, length us, event | category | flops | bytes accessed | tf_op | source)
XLA Modules:
  0.0 227.4 jit_solution(14979115997876258393)
XLA Ops:
  1.1 138.7 %while.16 = (s32[]{:T(128)}, f32[64,2048]{1,0:T(8,128)S(1)}, bf16[64,6144]{1,0:T(8,128)(2,1)}, f32[6,1024]{1,0:T(8,128)S(1)}, f32[6,1024]{1,0:T(8,128)S(1)}, /*i...) while((s32[]{:T(128)}, f32[64,2048]{1,0:T(8,128)S(1)}, ...), condition=%wide.region_1.2_spmd.clone.clone.clone, body=%wide.region_0.1_spmd.clone.clone.clone.sunk | while | flops 297009152 | bytes 9597093 | solution.py:91
  1.2 20.5 %fusion.73 = (bf16[1024,1024]{1,0:T(8,128)(2,1)S(1)}, bf16[1024,1024]{1,0:T(8,128)(2,1)}) fusion(s32[1024]{0:T(1024)} %get-tuple-element.293, f32[1024]{0:T(1024)S(1)} %bitcast.88, f32[1024]{0:T(1024)S(1)} %bitcast.89), kind=kLoop, calls=%fused_computation.20.clone.1 | loop fusion | flops 19922944 | bytes 4206592 | tf_op jit(solution)/shard_map/convert
  21.7 2.6 %fusion.74 = f32[64,2048]{1,0:T(8,128)S(1)} fusion(bf16[1024,1024]{1,0:T(8,128)(2,1)} %get-tuple-element.266, bf16[1024,1024]{1,0:T(8,128)(2,1)S(1)} %get-tuple-element.267, f32[64,2048]{1,0:T(8,128)S(1)} %get-tuple-element.279, pred[]{:T(512)S(6)} %compare.5, bf16[64,6144]{1,0:T(8,128)(2,1)} %get-tuple-element.290, s32[]{:T(128)S(6)} %select_n.219), kind=kOutput, calls=%fused_computation.25.clone.1 | convolution fusion | flops 277086208 | bytes 5373957 | tf_op jit(solution)/shard_map/while/body/eval_jaxpr/dot_general | solution.py:88
  24.3 20.5 %fusion.73 = (bf16[1024,1024]{1,0:T(8,128)(2,1)S(1)}, bf16[1024,1024]{1,0:T(8,128)(2,1)}) fusion(s32[1024]{0:T(1024)} %get-tuple-element.293, f32[1024]{0:T(1024)S(1)} %bitcast.88, f32[1024]{0:T(1024)S(1)} %bitcast.89), kind=kLoop, calls=%fused_computation.20.clone.1 | loop fusion | flops 19922944 | bytes 4206592 | tf_op jit(solution)/shard_map/convert
  44.8 2.6 %fusion.74 = f32[64,2048]{1,0:T(8,128)S(1)} fusion(bf16[1024,1024]{1,0:T(8,128)(2,1)} %get-tuple-element.266, bf16[1024,1024]{1,0:T(8,128)(2,1)S(1)} %get-tuple-element.267, f32[64,2048]{1,0:T(8,128)S(1)} %get-tuple-element.279, pred[]{:T(512)S(6)} %compare.5, bf16[64,6144]{1,0:T(8,128)(2,1)} %get-tuple-element.290, s32[]{:T(128)S(6)} %select_n.219), kind=kOutput, calls=%fused_computation.25.clone.1 | convolution fusion | flops 277086208 | bytes 5373957 | tf_op jit(solution)/shard_map/while/body/eval_jaxpr/dot_general | solution.py:88
  47.4 20.5 %fusion.73 = (bf16[1024,1024]{1,0:T(8,128)(2,1)S(1)}, bf16[1024,1024]{1,0:T(8,128)(2,1)}) fusion(s32[1024]{0:T(1024)} %get-tuple-element.293, f32[1024]{0:T(1024)S(1)} %bitcast.88, f32[1024]{0:T(1024)S(1)} %bitcast.89), kind=kLoop, calls=%fused_computation.20.clone.1 | loop fusion | flops 19922944 | bytes 4206592 | tf_op jit(solution)/shard_map/convert
  67.9 2.6 %fusion.74 = f32[64,2048]{1,0:T(8,128)S(1)} fusion(bf16[1024,1024]{1,0:T(8,128)(2,1)} %get-tuple-element.266, bf16[1024,1024]{1,0:T(8,128)(2,1)S(1)} %get-tuple-element.267, f32[64,2048]{1,0:T(8,128)S(1)} %get-tuple-element.279, pred[]{:T(512)S(6)} %compare.5, bf16[64,6144]{1,0:T(8,128)(2,1)} %get-tuple-element.290, s32[]{:T(128)S(6)} %select_n.219), kind=kOutput, calls=%fused_computation.25.clone.1 | convolution fusion | flops 277086208 | bytes 5373957 | tf_op jit(solution)/shard_map/while/body/eval_jaxpr/dot_general | solution.py:88
  70.5 20.5 %fusion.73 = (bf16[1024,1024]{1,0:T(8,128)(2,1)S(1)}, bf16[1024,1024]{1,0:T(8,128)(2,1)}) fusion(s32[1024]{0:T(1024)} %get-tuple-element.293, f32[1024]{0:T(1024)S(1)} %bitcast.88, f32[1024]{0:T(1024)S(1)} %bitcast.89), kind=kLoop, calls=%fused_computation.20.clone.1 | loop fusion | flops 19922944 | bytes 4206592 | tf_op jit(solution)/shard_map/convert
  91.0 2.6 %fusion.74 = f32[64,2048]{1,0:T(8,128)S(1)} fusion(bf16[1024,1024]{1,0:T(8,128)(2,1)} %get-tuple-element.266, bf16[1024,1024]{1,0:T(8,128)(2,1)S(1)} %get-tuple-element.267, f32[64,2048]{1,0:T(8,128)S(1)} %get-tuple-element.279, pred[]{:T(512)S(6)} %compare.5, bf16[64,6144]{1,0:T(8,128)(2,1)} %get-tuple-element.290, s32[]{:T(128)S(6)} %select_n.219), kind=kOutput, calls=%fused_computation.25.clone.1 | convolution fusion | flops 277086208 | bytes 5373957 | tf_op jit(solution)/shard_map/while/body/eval_jaxpr/dot_general | solution.py:88
  93.7 20.5 %fusion.73 = (bf16[1024,1024]{1,0:T(8,128)(2,1)S(1)}, bf16[1024,1024]{1,0:T(8,128)(2,1)}) fusion(s32[1024]{0:T(1024)} %get-tuple-element.293, f32[1024]{0:T(1024)S(1)} %bitcast.88, f32[1024]{0:T(1024)S(1)} %bitcast.89), kind=kLoop, calls=%fused_computation.20.clone.1 | loop fusion | flops 19922944 | bytes 4206592 | tf_op jit(solution)/shard_map/convert
  114.2 2.6 %fusion.74 = f32[64,2048]{1,0:T(8,128)S(1)} fusion(bf16[1024,1024]{1,0:T(8,128)(2,1)} %get-tuple-element.266, bf16[1024,1024]{1,0:T(8,128)(2,1)S(1)} %get-tuple-element.267, f32[64,2048]{1,0:T(8,128)S(1)} %get-tuple-element.279, pred[]{:T(512)S(6)} %compare.5, bf16[64,6144]{1,0:T(8,128)(2,1)} %get-tuple-element.290, s32[]{:T(128)S(6)} %select_n.219), kind=kOutput, calls=%fused_computation.25.clone.1 | convolution fusion | flops 277086208 | bytes 5373957 | tf_op jit(solution)/shard_map/while/body/eval_jaxpr/dot_general | solution.py:88
  116.8 20.5 %fusion.73 = (bf16[1024,1024]{1,0:T(8,128)(2,1)S(1)}, bf16[1024,1024]{1,0:T(8,128)(2,1)}) fusion(s32[1024]{0:T(1024)} %get-tuple-element.293, f32[1024]{0:T(1024)S(1)} %bitcast.88, f32[1024]{0:T(1024)S(1)} %bitcast.89), kind=kLoop, calls=%fused_computation.20.clone.1 | loop fusion | flops 19922944 | bytes 4206592 | tf_op jit(solution)/shard_map/convert
  137.3 2.6 %fusion.74 = f32[64,2048]{1,0:T(8,128)S(1)} fusion(bf16[1024,1024]{1,0:T(8,128)(2,1)} %get-tuple-element.266, bf16[1024,1024]{1,0:T(8,128)(2,1)S(1)} %get-tuple-element.267, f32[64,2048]{1,0:T(8,128)S(1)} %get-tuple-element.279, pred[]{:T(512)S(6)} %compare.5, bf16[64,6144]{1,0:T(8,128)(2,1)} %get-tuple-element.290, s32[]{:T(128)S(6)} %select_n.219), kind=kOutput, calls=%fused_computation.25.clone.1 | convolution fusion | flops 277086208 | bytes 5373957 | tf_op jit(solution)/shard_map/while/body/eval_jaxpr/dot_general | solution.py:88
  142.2 2.2 reshape.161
  144.5 11.4 %all_to_all.18 = f32[4,1,32768]{2,1,0:T(1,128)S(1)} all-to-all(f32[4,1,32768]{2,1,0:T(1,128)S(1)} %reshape.161), channel_id=1, replica_groups=mesh['chan'=8,'win'=4] {'win'}, dimensions={0} | all-to-all | bytes 1048576 | tf_op jit(solution)/shard_map/all_to_all | solution.py:96
  168.4 2.3 copy.38
  172.1 4.4 %collective-permute-done = f32[8,32,2,256]{3,1,2,0:T(8,128)} collective-permute-done((f32[8,32,2,256]{3,1,2,0:T(8,128)S(1)}, f32[8,32,2,256]{3,1,2,0:T(8,128)}, u32[]{:S(2)}, u32[]{:S(2)}) %collective-permute-start) | collective-permute-done | bytes 524320 | tf_op jit(solution)/shard_map/ppermute | solution.py:16
  176.5 3.9 %copy.39 = f32[256,32,8,2]{1,3,2,0:T(2,128)} copy(f32[256,32,8,2]{0,1,3,2:T(8,128)} %bitcast.13) | data formatting | bytes 1048576 | tf_op jit(solution)/shard_map/transpose | solution.py:51
  180.4 7.1 %collective-permute-done.1 = f32[8,32,2,256]{3,1,2,0:T(8,128)S(1)} collective-permute-done((f32[8,32,2,256]{3,1,2,0:T(8,128)S(1)}, f32[8,32,2,256]{3,1,2,0:T(8,128)S(1)}, u32[]{:S(2)}, u32[]{:S(2)}) %collective-permute-start.1) | collective-permute-done | bytes 524320 | tf_op jit(solution)/shard_map/ppermute | solution.py:16
  187.6 2.4 %copy.40 = f32[256,32,8,2]{1,3,2,0:T(2,128)} copy(f32[256,32,8,2]{0,1,3,2:T(8,128)S(1)} %bitcast.87) | data formatting | bytes 1048576 | tf_op jit(solution)/shard_map/transpose | solution.py:51
  190.0 18.9 %broadcast_multiply_fusion = f32[256,64,96]{2,1,0:T(8,128)} fusion(f32[256,32,16]{1,2,0:T(8,128)} %bitcast.76, f32[256,32,16]{1,2,0:T(8,128)S(1)} %bitcast.75, f32[256,32,16]{1,2,0:T(8,128)} %bitcast.78, f32[256,32,16]{1,2,0:T(8,128)} %bitcast.77), kind=kOutput, calls=%fused_computation.32 | convolution fusion | flops 304611328 | bytes 8388608 | tf_op jit(solution)/shard_map/fik,fjk->fij/dot_general | solution.py:61
  208.9 8.5 %copy.41 = f32[256,64,96]{0,2,1:T(8,128)} copy(f32[256,64,96]{2,1,0:T(8,128)} %broadcast_multiply_fusion) | data formatting | bytes 12582912 | tf_op jit(solution)/shard_map/div | solution.py:61
  217.4 3.7 %select_bitcast_fusion = f32[1,256,2,32,32]{1,4,3,2,0:T(8,128)S(1)} fusion(f32[256,2,32,3,32]{0,4,3,2,1:T(8,128)} %bitcast.73, pred[]{:T(512)} %bitcast.27, pred[]{:T(512)} %bitcast.25), kind=kLoop, calls=%fused_computation.51 | loop fusion | flops 1048576 | bytes 8388610 | tf_op jit(solution)/shard_map/jit(_where)/select_n | solution.py:67
  223.9 3.5 %copy.48 = f32[32,3,2,32,256]{4,3,2,1,0:T(8,128)} copy(f32[32,3,2,32,256]{4,3,0,2,1:T(8,128)S(1)} %maximum_bitcast_fusion) | data formatting | bytes 12582912 | tf_op jit(solution)/shard_map/transpose | solution.py:74
  (30 shorter events, 16.6 us)
Async XLA Ops:
  144.5 19.5 %copy-start.1 = (s32[1,3]{1,0:T(1,128)S(1)}, s32[1,3]{1,0:T(1,128)}, u32[]{:S(2)}) copy-start(s32[1,3]{1,0:T(1,128)} %param.6) | copy-start | bytes 40
  161.2 15.3 %collective-permute-start = (f32[8,32,2,256]{3,1,2,0:T(8,128)S(1)}, f32[8,32,2,256]{3,1,2,0:T(8,128)}, u32[]{:S(2)}, u32[]{:S(2)}) collective-permute-start(f32[8,32,2,256]{3,1,2,0:T(8,128)S(1)} %bitcast.81), channel_id=1, source_target_pairs={{0,4},{4,8},{8,12},{12,16},{16,20},{20,24},{24,28},{1,5},{5,9},{9,... | collective-permute-start | bytes 1572872 | tf_op jit(solution)/shard_map/ppermute | solution.py:16
  162.5 25.1 %collective-permute-start.1 = (f32[8,32,2,256]{3,1,2,0:T(8,128)S(1)}, f32[8,32,2,256]{3,1,2,0:T(8,128)S(1)}, u32[]{:S(2)}, u32[]{:S(2)}) collective-permute-start(f32[8,32,2,256]{3,1,2,0:T(8,128)S(1)} %bitcast.82), channel_id=1, source_target_pairs={{0,8},{4,12},{8,16},{12,20},{16,24},{20,28},{1,9},{5,13},{9,17},{1... | collective-permute-start | bytes 1572872 | tf_op jit(solution)/shard_map/ppermute | solution.py:16
  217.4 4.7 %copy-start = (f32[256,64,96]{0,2,1:T(8,128)S(1)}, f32[256,64,96]{0,2,1:T(8,128)}, u32[]{:S(2)}) copy-start(f32[256,64,96]{0,2,1:T(8,128)} %copy.41) | copy-start | bytes 18874372
where the time goes:
time: 228 us; the launch traced here: 227 us
  other arithmetic  132 us (58%)
  matrix products  35.3 us (15%)
  local copies, waits for them, and re-layouts  30.5 us (13%)
  waiting for transfers between devices  11.5 us (5%)
  blocking collectives  11.4 us (5%)
  between operations  3.83 us (2%)
  starting transfers between devices  2.76 us (1%)
    another operation x6, other arithmetic  123 us
    dot_general x1, matrix products, pair_blocks(): jnp.einsum('fik,fjk->fij', left, right, precision=lax.Precision.HIGHEST)  18.9 us
    dot_general x6, matrix products, add_block(): return total + jnp.dot(piece, table, preferred_element_type=jnp.float32)  15.5 us
    ppermute x2, waiting for transfers between devices, passed_along(): lax.ppermute(value, axis, [(source, source + steps) for source in range(l...  11.5 us
    all_to_all x1, blocking collectives, shards(): lax.all_to_all(whitened, 'win', split_axis=3, concat_axis=0, tiled=True)  11.4 us
    transpose x4, local copies, waits for them, and re-layouts, arrange(): field.transpose(3, 1, 0, 2).reshape(freq_count, chan_count, win_count * 2)  10.1 us
    div x1, local copies, waits for them, and re-layouts, pair_blocks(): jnp.einsum('fik,fjk->fij', left, right, precision=lax.Precision.HIGHEST)  8.54 us
    unnamed x6, local copies, waits for them, and re-layouts  4.95 us
  transfers between devices with their start and end apart: 2, of which 2 were waited for; matrix products, arithmetic and copies ran while one was open for 4% of the time, Pallas kernels for 0%

commit v1 on v0

--- a/solution.py
+++ b/solution.py
@@ -8,6 +8,28 @@
 HALF = 64
 TB = 1024
 EPSILON = 1e-06
+
+
+def split_up(x, dim, size):
+    before, after = (x.shape[:dim], x.shape[dim + 1 :])
+    return jnp.moveaxis(x.reshape(*before, size, -1, *after), dim, 0)
+
+
+def laid_out(blocks, dim):
+    dims = list(blocks.shape[1:])
+    dims[dim] *= blocks.shape[0]
+    return jnp.moveaxis(blocks, 0, dim).reshape(dims)
+
+
+def swapped_with_each(value, axis, split_dim, concat_dim):
+    size, mine = (lax.axis_size(axis), lax.axis_index(axis))
+    blocks = split_up(value, split_dim, size)
+    outs = [blocks[mine]]
+    for step in range(1, size):
+        sent = blocks[mine ^ step]
+        outs.append(lax.ppermute(sent, axis, [(i, i ^ step) for i in range(size)]))
+    blocks = jnp.stack(outs)[mine ^ jnp.arange(size)]
+    return laid_out(blocks, concat_dim)
 
 
 def passed_along(value, axis, steps):
@@ -93,7 +115,7 @@
     spectra = spectra.reshape(win_count, sensor_total, 2, freq_count)
     whitened = whiten(spectra, HALF)
     offsets = pair_offsets[0]
-    slabs = lax.all_to_all(whitened, "win", split_axis=3, concat_axis=0, tiled=True)
+    slabs = swapped_with_each(whitened, "win", 3, 0)
     return pair_blocks(slabs, offsets, slabs.shape[0])
 
 

time: 228 us -> 218 us (0.956)
  blocking collectives: 11.4 us -> 0 us
  waiting for transfers between devices: 11.5 us -> 18.4 us
  local copies, waits for them, and re-layouts: 30.5 us -> 24.8 us
    all_to_all x1 -> x0, blocking collectives: 11.4 us -> none  [shards(): lax.all_to_all(whitened, 'win', split_axis=3, concat_axis=0, tiled=True)]
    ppermute x0 -> x3, waiting for transfers between devices: none -> 6.45 us  [swapped_with_each(): outs.append(lax.ppermute(sent, axis, [(i, i ^ step) for i in range(size)]))]
    unnamed x6 -> x4, local copies, waits for them, and re-layouts: 4.95 us -> 0.93 us
    another operation x6 -> x7, other arithmetic: 123 us -> 123 us
  transfers between devices with their start and end apart: 2 -> 5, of which waited for: 2 -> 4; matrix products, arithmetic and copies ran while one was open for 4% -> 4% of each run, Pallas kernels for 0% -> 0%
where the time goes in v1:
time: 218 us
  other arithmetic  130 us (60%)
  matrix products  35.3 us (16%)
  local copies, waits for them, and re-layouts  24.8 us (11%)
  waiting for transfers between devices  18.4 us (8%)
  starting transfers between devices  4.97 us (2%)
  between operations  3.94 us (2%)
    another operation x6, other arithmetic  123 us
    dot_general x1, matrix products, pair_blocks(): jnp.einsum('fik,fjk->fij', left, right, precision=lax.Precision.HIGHEST)  18.9 us
    dot_general x6, matrix products, add_block(): return total + jnp.dot(piece, table, preferred_element_type=jnp.float32)  15.5 us
    ppermute x2, waiting for transfers between devices, passed_along(): lax.ppermute(value, axis, [(source, source + steps) for source in range(l...  12 us
    transpose x4, local copies, waits for them, and re-layouts, arrange(): field.transpose(3, 1, 0, 2).reshape(freq_count, chan_count, win_count * 2)  10.1 us
    div x1, local copies, waits for them, and re-layouts, pair_blocks(): jnp.einsum('fik,fjk->fij', left, right, precision=lax.Precision.HIGHEST)  8.54 us
    ppermute x3, waiting for transfers between devices, swapped_with_each(): outs.append(lax.ppermute(sent, axis, [(i, i ^ step) for i in range(size)]))  6.45 us
    select_n x2, other arithmetic, pair_blocks(): jnp.where(chosen == 0, joined[:, :, :, 0], jnp.where(chosen == 1, joined[...  4.45 us
  transfers between devices with their start and end apart: 5, of which 4 were waited for; matrix products, arithmetic and copies ran while one was open for 4% of the time, Pallas kernels for 0%

profile of v1, /device:TPU:28, one launch (start us, length us, event | category | flops | bytes accessed | tf_op | source)
XLA Modules:
  0.0 217.5 jit_solution(15391389886320443147)
XLA Ops:
  1.1 138.7 %while.16 = (s32[]{:T(128)}, f32[64,2048]{1,0:T(8,128)S(1)}, bf16[64,6144]{1,0:T(8,128)(2,1)}, f32[6,1024]{1,0:T(8,128)S(1)}, f32[6,1024]{1,0:T(8,128)S(1)}, /*i...) while((s32[]{:T(128)}, f32[64,2048]{1,0:T(8,128)S(1)}, ...), condition=%wide.region_1.2_spmd.clone.clone.clone, body=%wide.region_0.1_spmd.clone.clone.clone.sunk | while | flops 297009152 | bytes 9597093 | solution.py:113
  1.2 20.5 %fusion.74 = (bf16[1024,1024]{1,0:T(8,128)(2,1)S(1)}, bf16[1024,1024]{1,0:T(8,128)(2,1)}) fusion(s32[1024]{0:T(1024)} %get-tuple-element.297, f32[1024]{0:T(1024)S(1)} %bitcast.95, f32[1024]{0:T(1024)S(1)} %bitcast.96), kind=kLoop, calls=%fused_computation.21.clone.1 | loop fusion | flops 19922944 | bytes 4206592 | tf_op jit(solution)/shard_map/convert
  21.7 2.6 %fusion.75 = f32[64,2048]{1,0:T(8,128)S(1)} fusion(bf16[1024,1024]{1,0:T(8,128)(2,1)} %get-tuple-element.270, bf16[1024,1024]{1,0:T(8,128)(2,1)S(1)} %get-tuple-element.271, f32[64,2048]{1,0:T(8,128)S(1)} %get-tuple-element.283, pred[]{:T(512)S(6)} %compare.5, bf16[64,6144]{1,0:T(8,128)(2,1)} %get-tuple-element.294, s32[]{:T(128)S(6)} %select_n.249), kind=kOutput, calls=%fused_computation.26.clone.1 | convolution fusion | flops 277086208 | bytes 5373957 | tf_op jit(solution)/shard_map/while/body/eval_jaxpr/dot_general | solution.py:110
  24.3 20.5 %fusion.74 = (bf16[1024,1024]{1,0:T(8,128)(2,1)S(1)}, bf16[1024,1024]{1,0:T(8,128)(2,1)}) fusion(s32[1024]{0:T(1024)} %get-tuple-element.297, f32[1024]{0:T(1024)S(1)} %bitcast.95, f32[1024]{0:T(1024)S(1)} %bitcast.96), kind=kLoop, calls=%fused_computation.21.clone.1 | loop fusion | flops 19922944 | bytes 4206592 | tf_op jit(solution)/shard_map/convert
  44.8 2.6 %fusion.75 = f32[64,2048]{1,0:T(8,128)S(1)} fusion(bf16[1024,1024]{1,0:T(8,128)(2,1)} %get-tuple-element.270, bf16[1024,1024]{1,0:T(8,128)(2,1)S(1)} %get-tuple-element.271, f32[64,2048]{1,0:T(8,128)S(1)} %get-tuple-element.283, pred[]{:T(512)S(6)} %compare.5, bf16[64,6144]{1,0:T(8,128)(2,1)} %get-tuple-element.294, s32[]{:T(128)S(6)} %select_n.249), kind=kOutput, calls=%fused_computation.26.clone.1 | convolution fusion | flops 277086208 | bytes 5373957 | tf_op jit(solution)/shard_map/while/body/eval_jaxpr/dot_general | solution.py:110
  47.4 20.5 %fusion.74 = (bf16[1024,1024]{1,0:T(8,128)(2,1)S(1)}, bf16[1024,1024]{1,0:T(8,128)(2,1)}) fusion(s32[1024]{0:T(1024)} %get-tuple-element.297, f32[1024]{0:T(1024)S(1)} %bitcast.95, f32[1024]{0:T(1024)S(1)} %bitcast.96), kind=kLoop, calls=%fused_computation.21.clone.1 | loop fusion | flops 19922944 | bytes 4206592 | tf_op jit(solution)/shard_map/convert
  67.9 2.6 %fusion.75 = f32[64,2048]{1,0:T(8,128)S(1)} fusion(bf16[1024,1024]{1,0:T(8,128)(2,1)} %get-tuple-element.270, bf16[1024,1024]{1,0:T(8,128)(2,1)S(1)} %get-tuple-element.271, f32[64,2048]{1,0:T(8,128)S(1)} %get-tuple-element.283, pred[]{:T(512)S(6)} %compare.5, bf16[64,6144]{1,0:T(8,128)(2,1)} %get-tuple-element.294, s32[]{:T(128)S(6)} %select_n.249), kind=kOutput, calls=%fused_computation.26.clone.1 | convolution fusion | flops 277086208 | bytes 5373957 | tf_op jit(solution)/shard_map/while/body/eval_jaxpr/dot_general | solution.py:110
  70.6 20.5 %fusion.74 = (bf16[1024,1024]{1,0:T(8,128)(2,1)S(1)}, bf16[1024,1024]{1,0:T(8,128)(2,1)}) fusion(s32[1024]{0:T(1024)} %get-tuple-element.297, f32[1024]{0:T(1024)S(1)} %bitcast.95, f32[1024]{0:T(1024)S(1)} %bitcast.96), kind=kLoop, calls=%fused_computation.21.clone.1 | loop fusion | flops 19922944 | bytes 4206592 | tf_op jit(solution)/shard_map/convert
  91.0 2.6 %fusion.75 = f32[64,2048]{1,0:T(8,128)S(1)} fusion(bf16[1024,1024]{1,0:T(8,128)(2,1)} %get-tuple-element.270, bf16[1024,1024]{1,0:T(8,128)(2,1)S(1)} %get-tuple-element.271, f32[64,2048]{1,0:T(8,128)S(1)} %get-tuple-element.283, pred[]{:T(512)S(6)} %compare.5, bf16[64,6144]{1,0:T(8,128)(2,1)} %get-tuple-element.294, s32[]{:T(128)S(6)} %select_n.249), kind=kOutput, calls=%fused_computation.26.clone.1 | convolution fusion | flops 277086208 | bytes 5373957 | tf_op jit(solution)/shard_map/while/body/eval_jaxpr/dot_general | solution.py:110
  93.7 20.5 %fusion.74 = (bf16[1024,1024]{1,0:T(8,128)(2,1)S(1)}, bf16[1024,1024]{1,0:T(8,128)(2,1)}) fusion(s32[1024]{0:T(1024)} %get-tuple-element.297, f32[1024]{0:T(1024)S(1)} %bitcast.95, f32[1024]{0:T(1024)S(1)} %bitcast.96), kind=kLoop, calls=%fused_computation.21.clone.1 | loop fusion | flops 19922944 | bytes 4206592 | tf_op jit(solution)/shard_map/convert
  114.2 2.6 %fusion.75 = f32[64,2048]{1,0:T(8,128)S(1)} fusion(bf16[1024,1024]{1,0:T(8,128)(2,1)} %get-tuple-element.270, bf16[1024,1024]{1,0:T(8,128)(2,1)S(1)} %get-tuple-element.271, f32[64,2048]{1,0:T(8,128)S(1)} %get-tuple-element.283, pred[]{:T(512)S(6)} %compare.5, bf16[64,6144]{1,0:T(8,128)(2,1)} %get-tuple-element.294, s32[]{:T(128)S(6)} %select_n.249), kind=kOutput, calls=%fused_computation.26.clone.1 | convolution fusion | flops 277086208 | bytes 5373957 | tf_op jit(solution)/shard_map/while/body/eval_jaxpr/dot_general | solution.py:110
  116.8 20.5 %fusion.74 = (bf16[1024,1024]{1,0:T(8,128)(2,1)S(1)}, bf16[1024,1024]{1,0:T(8,128)(2,1)}) fusion(s32[1024]{0:T(1024)} %get-tuple-element.297, f32[1024]{0:T(1024)S(1)} %bitcast.95, f32[1024]{0:T(1024)S(1)} %bitcast.96), kind=kLoop, calls=%fused_computation.21.clone.1 | loop fusion | flops 19922944 | bytes 4206592 | tf_op jit(solution)/shard_map/convert
  137.3 2.6 %fusion.75 = f32[64,2048]{1,0:T(8,128)S(1)} fusion(bf16[1024,1024]{1,0:T(8,128)(2,1)} %get-tuple-element.270, bf16[1024,1024]{1,0:T(8,128)(2,1)S(1)} %get-tuple-element.271, f32[64,2048]{1,0:T(8,128)S(1)} %get-tuple-element.283, pred[]{:T(512)S(6)} %compare.5, bf16[64,6144]{1,0:T(8,128)(2,1)} %get-tuple-element.294, s32[]{:T(128)S(6)} %select_n.249), kind=kOutput, calls=%fused_computation.26.clone.1 | convolution fusion | flops 277086208 | bytes 5373957 | tf_op jit(solution)/shard_map/while/body/eval_jaxpr/dot_general | solution.py:110
  143.6 3.6 %collective-permute-done.2 = f32[2,32,2,256]{3,1,2,0:T(8,128)S(1)} collective-permute-done((f32[2,32,2,256]{3,1,2,0:T(8,128)S(1)}, f32[2,32,2,256]{3,1,2,0:T(8,128)S(1)}, u32[]{:S(2)}, u32[]{:S(2)}) %collective-permute-start.2) | collective-permute-done | bytes 131104 | tf_op jit(solution)/shard_map/ppermute | solution.py:30
  147.2 2.8 %collective-permute-done.1 = f32[2,32,2,256]{3,1,2,0:T(8,128)S(1)} collective-permute-done((f32[2,32,2,256]{3,1,2,0:T(8,128)S(1)}, f32[2,32,2,256]{3,1,2,0:T(8,128)S(1)}, u32[]{:S(2)}, u32[]{:S(2)}) %collective-permute-start.1) | collective-permute-done | bytes 131104 | tf_op jit(solution)/shard_map/ppermute | solution.py:30
  158.0 2.3 %copy.29 = f32[256,32,8,2]{1,3,2,0:T(2,128)} copy(f32[256,32,8,2]{0,1,3,2:T(8,128)S(1)} %maximum_bitcast_fusion.1) | data formatting | bytes 1048576 | tf_op jit(solution)/shard_map/transpose | solution.py:73
  161.8 4.8 %collective-permute-done.3 = f32[8,32,2,256]{3,1,2,0:T(8,128)} collective-permute-done((f32[8,32,2,256]{3,1,2,0:T(8,128)S(1)}, f32[8,32,2,256]{3,1,2,0:T(8,128)}, u32[]{:S(2)}, u32[]{:S(2)}) %collective-permute-start.3) | collective-permute-done | bytes 524320 | tf_op jit(solution)/shard_map/ppermute | solution.py:38
  166.6 3.9 %copy.30 = f32[256,32,8,2]{1,3,2,0:T(2,128)} copy(f32[256,32,8,2]{0,1,3,2:T(8,128)} %bitcast.17) | data formatting | bytes 1048576 | tf_op jit(solution)/shard_map/transpose | solution.py:73
  170.5 7.1 %collective-permute-done.4 = f32[8,32,2,256]{3,1,2,0:T(8,128)S(1)} collective-permute-done((f32[8,32,2,256]{3,1,2,0:T(8,128)S(1)}, f32[8,32,2,256]{3,1,2,0:T(8,128)S(1)}, u32[]{:S(2)}, u32[]{:S(2)}) %collective-permute-start.4) | collective-permute-done | bytes 524320 | tf_op jit(solution)/shard_map/ppermute | solution.py:38
  177.7 2.4 %copy.31 = f32[256,32,8,2]{1,3,2,0:T(2,128)} copy(f32[256,32,8,2]{0,1,3,2:T(8,128)S(1)} %bitcast.94) | data formatting | bytes 1048576 | tf_op jit(solution)/shard_map/transpose | solution.py:73
  180.0 18.9 %broadcast_multiply_fusion = f32[256,64,96]{2,1,0:T(8,128)} fusion(f32[256,32,16]{1,2,0:T(8,128)} %bitcast.86, f32[256,32,16]{1,2,0:T(8,128)S(1)} %bitcast.85, f32[256,32,16]{1,2,0:T(8,128)} %bitcast.88, f32[256,32,16]{1,2,0:T(8,128)} %bitcast.87), kind=kOutput, calls=%fused_computation.33 | convolution fusion | flops 304611328 | bytes 8388608 | tf_op jit(solution)/shard_map/fik,fjk->fij/dot_general | solution.py:83
  199.0 8.5 %copy.32 = f32[256,64,96]{0,2,1:T(8,128)} copy(f32[256,64,96]{2,1,0:T(8,128)} %broadcast_multiply_fusion) | data formatting | bytes 12582912 | tf_op jit(solution)/shard_map/div | solution.py:83
  207.5 3.7 %select_bitcast_fusion = f32[1,256,2,32,32]{1,4,3,2,0:T(8,128)S(1)} fusion(f32[256,2,32,3,32]{0,4,3,2,1:T(8,128)} %bitcast.83, pred[]{:T(512)} %bitcast.31, pred[]{:T(512)} %bitcast.29), kind=kLoop, calls=%fused_computation.52 | loop fusion | flops 1048576 | bytes 8388610 | tf_op jit(solution)/shard_map/jit(_where)/select_n | solution.py:89
  214.0 3.5 %copy.39 = f32[32,3,2,32,256]{4,3,2,1,0:T(8,128)} copy(f32[32,3,2,32,256]{4,3,0,2,1:T(8,128)S(1)} %maximum_bitcast_fusion) | data formatting | bytes 12582912 | tf_op jit(solution)/shard_map/transpose | solution.py:96
  (39 shorter events, 13.2 us)
Async XLA Ops:
  140.8 12.7 %copy-start.1 = (s32[1,3]{1,0:T(1,128)S(1)}, s32[1,3]{1,0:T(1,128)}, u32[]{:S(2)}) copy-start(s32[1,3]{1,0:T(1,128)} %param.6) | copy-start | bytes 40
  141.4 5.8 %collective-permute-start.2 = (f32[2,32,2,256]{3,1,2,0:T(8,128)S(1)}, f32[2,32,2,256]{3,1,2,0:T(8,128)S(1)}, u32[]{:S(2)}, u32[]{:S(2)}) collective-permute-start(f32[2,32,2,256]{3,1,2,0:T(8,128)S(1)} %get-tuple-element.216), channel_id=1, source_target_pairs={{0,3},{1,2},{2,1},{3,0},{4,7},{5,6},{6,5},{7,4},{8,11},{9,10},{10,... | collective-permute-start | bytes 393224 | tf_op jit(solution)/shard_map/ppermute | solution.py:30
  142.4 4.8 %collective-permute-start = (f32[2,32,2,256]{3,1,2,0:T(8,128)S(1)}, f32[2,32,2,256]{3,1,2,0:T(8,128)S(1)}, u32[]{:S(2)}, u32[]{:S(2)}) collective-permute-start(f32[2,32,2,256]{3,1,2,0:T(8,128)S(1)} %get-tuple-element.218), channel_id=1, source_target_pairs={{0,1},{1,0},{2,3},{3,2},{4,5},{5,4},{6,7},{7,6},{8,9},{9,8},{10,11... | collective-permute-start | bytes 393224 | tf_op jit(solution)/shard_map/ppermute | solution.py:30
  143.1 7.0 %collective-permute-start.1 = (f32[2,32,2,256]{3,1,2,0:T(8,128)S(1)}, f32[2,32,2,256]{3,1,2,0:T(8,128)S(1)}, u32[]{:S(2)}, u32[]{:S(2)}) collective-permute-start(f32[2,32,2,256]{3,1,2,0:T(8,128)S(1)} %get-tuple-element.217), channel_id=1, source_target_pairs={{0,2},{1,3},{2,0},{3,1},{4,6},{5,7},{6,4},{7,5},{8,10},{9,11},{10,... | collective-permute-start | bytes 393224 | tf_op jit(solution)/shard_map/ppermute | solution.py:30
  150.7 15.9 %collective-permute-start.3 = (f32[8,32,2,256]{3,1,2,0:T(8,128)S(1)}, f32[8,32,2,256]{3,1,2,0:T(8,128)}, u32[]{:S(2)}, u32[]{:S(2)}) collective-permute-start(f32[8,32,2,256]{3,1,2,0:T(8,128)S(1)} %bitcast.89), channel_id=1, source_target_pairs={{0,4},{4,8},{8,12},{12,16},{16,20},{20,24},{24,28},{1,5},{5,9},{9,... | collective-permute-start | bytes 1572872 | tf_op jit(solution)/shard_map/ppermute | solution.py:38
  152.0 25.7 %collective-permute-start.4 = (f32[8,32,2,256]{3,1,2,0:T(8,128)S(1)}, f32[8,32,2,256]{3,1,2,0:T(8,128)S(1)}, u32[]{:S(2)}, u32[]{:S(2)}) collective-permute-start(f32[8,32,2,256]{3,1,2,0:T(8,128)S(1)} %bitcast.90), channel_id=1, source_target_pairs={{0,8},{4,12},{8,16},{12,20},{16,24},{20,28},{1,9},{5,13},{9,17},{1... | collective-permute-start | bytes 1572872 | tf_op jit(solution)/shard_map/ppermute | solution.py:38
  207.5 4.7 %copy-start = (f32[256,64,96]{0,2,1:T(8,128)S(1)}, f32[256,64,96]{0,2,1:T(8,128)}, u32[]{:S(2)}) copy-start(f32[256,64,96]{0,2,1:T(8,128)} %copy.32) | copy-start | bytes 18874372
